TPU v7x, 512 devices: a whole 4x4x16 slice. The times are simulated.
512 devices in a mesh: dp: 32 (over z, core), tensor: 16 (over y, x).
Axes of the slice: x: 4, y: 4, z: 16, core: 2. Of those that a mesh axis runs over, the one named last changes fastest.
Arguments:
- dout: bfloat16 [12288, 5120], P(('dp', 'tensor')), may hold values from -0.75 to 0.75
- attn_ctx: bfloat16 [12288, 5120], P('dp', 'tensor'), may hold values from -6 to 6
- mlp_hidden: bfloat16 [12288, 13824], P('dp', 'tensor'), may hold values from -6 to 6
- w_out: bfloat16 [5120, 5120], P('tensor', 'dp'), may hold values from -0.078125 to 0.078125
- w_down: bfloat16 [13824, 5120], P('tensor', 'dp'), may hold values from -0.0546875 to 0.0546875
- head_logits: float32 [40], replicated, may hold values from -2 to 3
- unit_logits: float32 [13824], P('tensor'), may hold values from -2 to 3
- head_noise: float32 [40], replicated, may hold values from 0.001 to 0.999
- unit_noise: float32 [13824], P('tensor'), may hold values from 0.001 to 0.999
- linear_mult: float32 [1], replicated, may hold values from 100 to 300
- square_mult: float32 [1], replicated, may hold values from 1 to 4
- target: float32 [1], replicated, may hold values from 40 to 70
Outputs:
- ctx_grad: bfloat16 [12288, 5120], P('dp', 'tensor')
- hidden_grad: bfloat16 [12288, 13824], P('dp', 'tensor')
- head_grad: float32 [40], replicated
- unit_grad: float32 [13824], P('tensor')
All inputs are finite; a program needn't handle non-finite values.
Results may differ from a plain program's by a relative error of at most 0.001.
Values may be sent and summed in bfloat16 or wider, within the bound.
No kernel may reach another device: no remote copies, remote signals or barrier semaphores. Data moves between devices by JAX's collectives and lax.ppermute only.
A program may use at most 64 MiB of HBM per device.

v0:
```python
import jax
import jax.numpy as jnp
from jax import lax
from jax.sharding import PartitionSpec as P

H = 40
HEAD = 128
FF = 13824


low_end = -0.1
high_end = 1.1
temper = 2.0 / 3.0


def concrete(logits, noise):
    shape_s = jax.nn.sigmoid((jnp.log(noise) - jnp.log(1.0 - noise) + logits) / temper)
    stretched = shape_s * (high_end - low_end) + low_end
    gate = jnp.clip(stretched, 0.0, 1.0)
    inside = jnp.logical_and(stretched > 0.0, stretched < 1.0)
    slope = jnp.where(
        inside, (high_end - low_end) / temper * shape_s * (1.0 - shape_s), 0.0 * shape_s
    )
    return (gate, slope)


def open_prob(logits):
    return jax.nn.sigmoid(logits - temper * jnp.log(-low_end / high_end))


def local(
    dout,
    attn_ctx,
    mlp_hidden,
    w_out,
    w_down,
    head_logits,
    unit_logits,
    head_noise,
    unit_noise,
    linear_mult,
    square_mult,
    target,
):
    head_gate, head_slope = concrete(head_logits, head_noise)
    unit_gate, unit_slope = concrete(unit_logits, unit_noise)
    col_count = attn_ctx.shape[1]
    head_total = head_logits.shape[0]
    tensor_index = lax.axis_index("tensor")
    columns = tensor_index * col_count + lax.iota(jnp.int32, col_count)
    owner = columns // HEAD
    member = (owner[:, None] == lax.iota(jnp.int32, head_total)[None, :]).astype(jnp.float32)
    col_gate = jnp.dot(member, head_gate, precision=lax.Precision.HIGHEST)
    full_rows = lax.all_gather(dout, "tensor", axis=0, tiled=True)
    dims = (((1,), (1,)), ((), ()))

    def contract(piece):
        return lax.dot_general(full_rows, piece, dims, preferred_element_type=jnp.float32)

    ctx_pre = contract(lax.all_gather(w_out, "dp", axis=1, tiled=True))
    hid_pre = contract(lax.all_gather(w_down, "dp", axis=1, tiled=True))
    ctx_grad = (ctx_pre * col_gate[None, :]).astype(jnp.bfloat16)
    hidden_grad = (hid_pre * unit_gate[None, :]).astype(jnp.bfloat16)
    col_part = jnp.sum(attn_ctx.astype(jnp.float32) * ctx_pre, axis=0)
    unit_part = jnp.sum(mlp_hidden.astype(jnp.float32) * hid_pre, axis=0)
    head_part = jnp.dot(col_part, member, precision=lax.Precision.HIGHEST)
    p_head = open_prob(head_logits)
    p_unit = open_prob(unit_logits)
    local_mass = jnp.sum(p_unit)
    unit_data = lax.psum(unit_part, "dp")
    head_data = lax.psum(head_part, ("dp", "tensor"))
    unit_mass = lax.psum(local_mass, "tensor")
    denom = 4.0 * HEAD * H + 3.0 * FF
    size = 100.0 * (4.0 * HEAD * jnp.sum(p_head) + 3.0 * unit_mass) / denom
    factor = linear_mult[0] + 2.0 * square_mult[0] * (size - target[0])
    head_grad = head_data * head_slope + factor * (400.0 * HEAD / denom) * p_head * (1.0 - p_head)
    unit_grad = unit_data * unit_slope + factor * (300.0 / denom) * p_unit * (1.0 - p_unit)
    return (ctx_grad, hidden_grad, head_grad, unit_grad)


def solution(mesh):
    placed = (
        P(("dp", "tensor"), None),
        P("dp", "tensor"),
        P("dp", "tensor"),
        P("tensor", "dp"),
        P("tensor", "dp"),
        P(),
        P("tensor"),
        P(),
        P("tensor"),
        P(),
        P(),
        P(),
    )
    return jax.shard_map(
        local,
        mesh=mesh,
        in_specs=placed,
        out_specs=(P("dp", "tensor"), P("dp", "tensor"), P(), P("tensor")),
        check_vma=False,
    )
```

profile of v0, /device:TPU:1, one launch (start us, length us, event | category | flops | bytes accessed | tf_op | source)
XLA Modules:
  0.0 329.6 jit_solution(5489138382124432926)
XLA Ops:
  7.2 0.0 all-gather.6.cloned.1.call-start
  7.2 0.7 all-gather.6.cloned.1.call-update
  7.9 0.0 all-gather.4.cloned.1.call-start
  7.9 0.7 all-gather.4.cloned.1.call-update
  8.6 0.0 all-gather.8.cloned.1.call-start
  8.7 0.7 all-gather.8.cloned.1.call-update
  9.4 1.3 fusion.2
  10.7 34.9 %psum.22 = f32[]{:T(128)} all-reduce(f32[]{:T(128)} %get-tuple-element.11), channel_id=1, replica_groups=mesh['dp'=32,'tensor'=16] {'tensor'}, use_global_device_ids=true, to_apply=%region_4.5 | all-reduce | flops 1 | bytes 8 | tf_op jit(solution)/shard_map/psum | solution.py:72
  48.2 1.3 fusion.17
  50.1 0.0 copy-start.2
  50.1 0.0 copy-start.3
  50.2 0.0 copy-start.4
  50.2 38.7 %all-gather.6.cloned.1.call-done = bf16[320,5120]{0,1:T(8,128)(2,1)} async-done(((bf16[320,160]{0,1:T(8,128)(2,1)}), bf16[320,5120]{0,1:T(8,128)(2,1)}) %all-gather.6.cloned.1.call-update) | async-done | bytes 3276816 | tf_op jit(solution)/shard_map/all_gather | solution.py:60
  88.8 65.0 %all-gather.4.cloned.1.call-done = bf16[384,5120]{1,0:T(8,128)(2,1)} async-done(((bf16[24,5120]{1,0:T(8,128)(2,1)}), bf16[384,5120]{1,0:T(8,128)(2,1)}) %all-gather.4.cloned.1.call-update) | async-done | bytes 3932176 | tf_op jit(solution)/shard_map/all_gather | solution.py:54
  153.9 5.3 %multiply_reduce_fusion.1 = (f32[320]{0:T(512)S(1)}, f32[384,320]{0,1:T(8,128)S(1)}) fusion(bf16[384,320]{0,1:T(8,128)(2,1)} %param.13, bf16[384,5120]{1,0:T(8,128)(2,1)} %all-gather.4.cloned.1.call-done, bf16[320,5120]{0,1:T(8,128)(2,1)} %all-gather.6.cloned.1.call-done), kind=kOutput, calls=%fused_computation.4 | convolution fusion | flops 1258659584 | bytes 7947520 | tf_op jit(solution)/shard_map/dot_general | solution.py:58
  159.2 0.2 convolution_bitcast_fusion
  159.5 105.0 %psum.21 = f32[40]{0:T(128)S(1)} all-reduce(f32[40]{0:T(128)S(1)} %convolution_bitcast_fusion), channel_id=1, replica_groups=mesh['dp'=32,'tensor'=16] {'dp','tensor'}, use_global_device_ids=true, to_apply=%region_1.2 | all-reduce | flops 40 | bytes 320 | tf_op jit(solution)/shard_map/psum | solution.py:71
  264.5 0.0 copy-done.2
  264.5 0.0 copy-done.3
  264.5 0.5 multiply_add_fusion.2
  265.0 0.3 convolution_reduce_fusion
  265.3 0.8 multiply_convert_fusion.1
  266.1 0.0 all-gather.8.cloned.1.call-done
  266.2 0.0 copy-done.4
  266.2 0.0 copy-start
  266.2 0.0 copy-start.1
  266.2 10.5 %multiply_reduce_fusion = (f32[864]{0:T(1024)S(1)}, bf16[384,864]{0,1:T(8,128)(2,1)}) fusion(bf16[384,864]{0,1:T(8,128)(2,1)S(1)} %copy-done.4, f32[864]{0:T(1024)S(1)} %get-tuple-element.10, bf16[384,5120]{1,0:T(8,128)(2,1)} %all-gather.4.cloned.1.call-done, bf16[864,5120]{0,1:T(8,128)(2,1)} %all-gather.8.cloned.1.call-done), kind=kOutput, calls=%fused_computation | convolution fusion | flops 3399044352 | bytes 14113536 | tf_op jit(solution)/shard_map/dot_general | solution.py:58
  276.7 45.8 %psum.23 = f32[864]{0:T(1024)S(1)} all-reduce(f32[864]{0:T(1024)S(1)} %get-tuple-element.8), channel_id=1, replica_groups=mesh['dp'=32,'tensor'=16] {'dp'}, use_global_device_ids=true, to_apply=%region_6.7 | all-reduce | flops 864 | bytes 6912 | tf_op jit(solution)/shard_map/psum | solution.py:70
  322.5 0.0 copy-done
  322.5 0.0 copy-done.1
  322.5 0.6 multiply_add_fusion
  (2 shorter events, 0.0 us)
Async XLA Ops:
  7.2 81.7 %all-gather.6.cloned.1.call-start = ((), (), s32[]{:S(2)}) async-start(), calls=%async_computation.1 | async-start | bytes 4055040 | tf_op jit(solution)/shard_map/all_gather | solution.py:60
  7.9 146.0 %all-gather.4.cloned.1.call-start = ((), (), s32[]{:S(2)}) async-start(), calls=%async_computation | async-start | bytes 4177920 | tf_op jit(solution)/shard_map/all_gather | solution.py:54
  8.6 257.5 %all-gather.8.cloned.1.call-start = ((), (), s32[]{:S(2)}) async-start(), calls=%async_computation.2 | async-start | bytes 9461760 | tf_op jit(solution)/shard_map/all_gather | solution.py:61
  50.1 214.4 %copy-start.2 = (f32[40]{0:T(128)S(1)}, f32[40]{0:T(128)}, u32[]{:S(2)}) copy-start(f32[40]{0:T(128)} %param.17) | copy-start | bytes 484
  50.1 214.4 %copy-start.3 = (f32[40]{0:T(128)S(1)}, f32[40]{0:T(128)}, u32[]{:S(2)}) copy-start(f32[40]{0:T(128)} %param.19) | copy-start | bytes 484
  50.2 216.0 %copy-start.4 = (bf16[384,864]{0,1:T(8,128)(2,1)S(1)}, bf16[384,864]{0,1:T(8,128)(2,1)}, u32[]{:S(2)}) copy-start(bf16[384,864]{0,1:T(8,128)(2,1)} %param.14) | copy-start | bytes 1990660
  266.2 56.3 %copy-start = (f32[864]{0:T(1024)S(1)}, f32[864]{0:T(1024)}, u32[]{:S(2)}) copy-start(f32[864]{0:T(1024)} %param.18) | copy-start | bytes 10372
  266.2 56.3 %copy-start.1 = (f32[864]{0:T(1024)S(1)}, f32[864]{0:T(1024)}, u32[]{:S(2)}) copy-start(f32[864]{0:T(1024)} %param.20) | copy-start | bytes 10372
Sparse Core Ops, SparseCore 0:
  10.1 78.6 all-gather.5
  91.8 61.9 all-gather.3
  156.0 80.5 all-gather.7
where the time goes:
time: 330 us
  blocking collectives  186 us (56%)
  waiting for transfers between devices  106 us (32%)
  between operations  17.1 us (5%)
  matrix products  16.4 us (5%)
  other arithmetic  4.6 us (1%)
    psum x1, blocking collectives, local(): head_data = lax.psum(head_part, ('dp', 'tensor'))  105 us
    all_gather x1, waiting for transfers between devices, local(): full_rows = lax.all_gather(dout, 'tensor', axis=0, tiled=True)  65 us
    psum x1, blocking collectives, local(): unit_data = lax.psum(unit_part, 'dp')  45.8 us
    all_gather x1, waiting for transfers between devices, local(): ctx_pre = contract(lax.all_gather(w_out, 'dp', axis=1, tiled=True))  38.7 us
    psum x1, blocking collectives, local(): unit_mass = lax.psum(local_mass, 'tensor')  34.9 us
    dot_general x2, matrix products, contract(): lax.dot_general(full_rows, piece, dims, preferred_element_type=jnp.float32)  15.9 us
  transfers between devices with their start and end apart: 3, of which 2 were waited for; matrix products, arithmetic and copies ran while one was open for 3% of the time, Pallas kernels for 0%

commit v1 on v0

v1 whole, which is shorter than its diff:
```python
import jax
import jax.numpy as jnp
from jax import lax
from jax.experimental import pallas as pl
from jax.experimental.pallas import tpu as pltpu
from jax.sharding import PartitionSpec as P

HEAD = 128
LANE = 128
TILE = 256

low_end = -0.1
high_end = 1.1
temper = 2.0 / 3.0


def concrete(logits, noise):
    shape_s = jax.nn.sigmoid((jnp.log(noise) - jnp.log(1.0 - noise) + logits) / temper)
    stretched = shape_s * (high_end - low_end) + low_end
    gate = jnp.clip(stretched, 0.0, 1.0)
    inside = jnp.logical_and(stretched > 0.0, stretched < 1.0)
    slope = jnp.where(
        inside, (high_end - low_end) / temper * shape_s * (1.0 - shape_s), 0.0 * shape_s
    )
    return (gate, slope)


def open_prob(logits):
    return jax.nn.sigmoid(logits - temper * jnp.log(-low_end / high_end))


def up(n, m):
    return -(-n // m) * m


def pad_to(x, n):
    return jnp.pad(x, ((0, 0), (0, n - x.shape[1])))


def pre_grads(rows, weight, act, gate, n_ctx, n_hid, copies):
    tokens, cols = act.shape
    depth = weight.shape[0]
    parts = len(rows)
    step_k = depth // parts
    hid_at = up(n_ctx, LANE)
    steps = cols // TILE

    def kernel(*refs):
        row_refs = refs[:parts]
        w_ref, act_ref, gate_ref, ctx_ref, hid_ref, sum_ref = refs[parts:]
        pre = jnp.zeros((tokens, TILE), jnp.float32)
        for q in range(parts):
            pre += jnp.dot(
                row_refs[q][...],
                w_ref[pl.ds(q * step_k, step_k), :],
                preferred_element_type=jnp.float32,
            )
        sums = jnp.sum(act_ref[...].astype(jnp.float32) * pre, axis=0, keepdims=True)
        sum_ref[...] = jnp.broadcast_to(sums, (copies, TILE))
        out = (pre * gate_ref[...]).astype(jnp.bfloat16).T
        j = pl.program_id(0)
        for s in range(steps):
            at = s * TILE

            @pl.when(j == s)
            def _():
                lo, hi = at, min(at + TILE, n_ctx)
                if hi > lo:
                    ctx_ref[pl.ds(lo, hi - lo), :] = out[lo - at : hi - at]
                lo, hi = max(at, hid_at), min(at + TILE, hid_at + n_hid)
                if hi > lo:
                    hid_ref[pl.ds(lo - hid_at, hi - lo), :] = out[lo - at : hi - at]

    whole = lambda shape: pl.BlockSpec(shape, lambda j: (0, 0))
    return pl.pallas_call(
        kernel,
        grid=(steps,),
        in_specs=[whole(r.shape) for r in rows]
        + [
            pl.BlockSpec((depth, TILE), lambda j: (0, j)),
            pl.BlockSpec((tokens, TILE), lambda j: (0, j)),
            pl.BlockSpec((1, TILE), lambda j: (0, j)),
        ],
        out_specs=[
            whole((n_ctx, tokens)),
            whole((n_hid, tokens)),
            pl.BlockSpec((copies, TILE), lambda j: (0, j)),
        ],
        out_shape=[
            jax.ShapeDtypeStruct((n_ctx, tokens), jnp.bfloat16),
            jax.ShapeDtypeStruct((n_hid, tokens), jnp.bfloat16),
            jax.ShapeDtypeStruct((copies, cols), jnp.float32),
        ],
        compiler_params=pltpu.CompilerParams(
            dimension_semantics=("arbitrary",), vmem_limit_bytes=56 * 2**20
        ),
        name="pre_grads",
    )(*rows, weight, act, gate)


def make_local(dp, tensor):
    side = 4
    along_x = [[b * side + i for i in range(side)] for b in range(tensor // side)]
    along_y = [[b + side * i for i in range(tensor // side)] for b in range(side)]

    def local(
        dout,
        attn_ctx,
        mlp_hidden,
        w_out,
        w_down,
        head_logits,
        unit_logits,
        head_noise,
        unit_noise,
        linear_mult,
        square_mult,
        target,
    ):
        n_ctx = attn_ctx.shape[1]
        n_hid = mlp_hidden.shape[1]
        p_ctx, p_hid = up(n_ctx, LANE), up(n_hid, LANE)
        heads = head_logits.shape[0]

        packed = jnp.concatenate([pad_to(w_out.T, p_ctx), pad_to(w_down.T, p_hid)], axis=1)
        weight = lax.all_gather(packed, "dp", axis=0, tiled=True)

        wide = lax.all_gather(dout, "tensor", axis=0, tiled=True, axis_index_groups=along_x)
        chunk = wide.shape[1] // 4
        rows = [
            lax.all_gather(
                wide[:, q * chunk : (q + 1) * chunk],
                "tensor",
                axis=0,
                tiled=True,
                axis_index_groups=along_y,
            )
            for q in range(4)
        ]

        head_gate, head_slope = concrete(head_logits, head_noise)
        unit_gate, unit_slope = concrete(unit_logits, unit_noise)
        tensor_index = lax.axis_index("tensor")
        columns = tensor_index * n_ctx + lax.iota(jnp.int32, n_ctx)
        owner = columns // HEAD
        member = (owner[:, None] == lax.iota(jnp.int32, heads)[None, :]).astype(jnp.float32)
        col_gate = jnp.dot(member, head_gate, precision=lax.Precision.HIGHEST)
        gate = jnp.concatenate(
            [pad_to(col_gate[None, :], p_ctx), pad_to(unit_gate[None, :], p_hid)], axis=1
        )
        act = jnp.concatenate([pad_to(attn_ctx, p_ctx), pad_to(mlp_hidden, p_hid)], axis=1)

        ctx_t, hid_t, sums = pre_grads(rows, weight, act, gate, n_ctx, n_hid, dp)

        data = jnp.sum(lax.all_to_all(sums, "dp", 0, 0, tiled=True), axis=0)
        unit_data = data[p_ctx : p_ctx + n_hid]
        head_part = jnp.dot(data[:n_ctx], member, precision=lax.Precision.HIGHEST)
        p_head = open_prob(head_logits)
        p_unit = open_prob(unit_logits)
        local_mass = jnp.sum(p_unit)
        mine = jnp.concatenate(
            [head_part, local_mass[None], jnp.zeros((LANE - heads - 1,), jnp.float32)]
        )
        both = jnp.sum(
            lax.all_to_all(jnp.broadcast_to(mine, (tensor, LANE)), "tensor", 0, 0, tiled=True),
            axis=0,
        )
        head_data, unit_mass = both[:heads], both[heads]

        denom = 4.0 * HEAD * heads + 3.0 * n_hid * tensor
        size = 100.0 * (4.0 * HEAD * jnp.sum(p_head) + 3.0 * unit_mass) / denom
        factor = linear_mult[0] + 2.0 * square_mult[0] * (size - target[0])
        head_grad = head_data * head_slope + factor * (400.0 * HEAD / denom) * p_head * (
            1.0 - p_head
        )
        unit_grad = unit_data * unit_slope + factor * (300.0 / denom) * p_unit * (1.0 - p_unit)
        return (ctx_t.T, hid_t.T, head_grad, unit_grad)

    return local


def solution(mesh):
    placed = (
        P(("dp", "tensor"), None),
        P("dp", "tensor"),
        P("dp", "tensor"),
        P("tensor", "dp"),
        P("tensor", "dp"),
        P(),
        P("tensor"),
        P(),
        P("tensor"),
        P(),
        P(),
        P(),
    )
    return jax.shard_map(
        make_local(mesh.shape["dp"], mesh.shape["tensor"]),
        mesh=mesh,
        in_specs=placed,
        out_specs=(P("dp", "tensor"), P("dp", "tensor"), P(), P("tensor")),
        check_vma=False,
    )
```

time: 330 us -> 169 us (0.51)
  blocking collectives: 186 us -> 92.6 us
  waiting for transfers between devices: 106 us -> 27.2 us
  matrix products: 16.4 us -> 0.51 us
  Pallas kernels: 0 us -> 11.5 us
  starting transfers between devices: 0.11 us -> 6.57 us
  local copies, waits for them, and re-layouts: 0.03 us -> 4.08 us
    psum x3 -> x0, blocking collectives: 186 us -> none  [the longest x1 105 us: local(): head_data = lax.psum(head_part, ('dp', 'tensor'))]
    all_gather x3 -> x1, waiting for transfers between devices: 104 us -> 23.4 us  [local(): weight = lax.all_gather(packed, 'dp', axis=0, tiled=True)]
    all_gather x0 -> x5, blocking collectives: none -> 66.6 us  [the longest x4 53.9 us: local(): lax.all_gather(wide[:, q * chunk:(q + 1) * chunk], 'tensor', axis=0, tile...]
    all_to_all x0 -> x1, blocking collectives: none -> 26 us  [local(): data = jnp.sum(lax.all_to_all(sums, 'dp', 0, 0, tiled=True), axis=0)]
    dot_general x3 -> x1, matrix products: 16.1 us -> 0.24 us  [local(): head_part = jnp.dot(data[:n_ctx], member, precision=lax.Precision.HIGHEST)]
    pallas_call x0 -> x1, Pallas kernels: none -> 11.5 us  [pre_grads(): pl.pallas_call(kernel, grid=(steps,), in_specs=[whole(r.shape) for r in r...]
    all_to_all x0 -> x1, starting transfers between devices: none -> 6.53 us  [local(): lax.all_to_all(jnp.broadcast_to(mine, (tensor, LANE)), 'tensor', 0, 0, ti...]
    concatenate x0 -> x4, other arithmetic: none -> 4.24 us  [the longest x1 1.85 us: local(): jnp.concatenate([pad_to(w_out.T, p_ctx), pad_to(w_down.T, p_hid)], axis=1)]
  transfers between devices with their start and end apart: 3 -> 2, of which waited for: 2 -> 2; matrix products, arithmetic and copies ran while one was open for 3% -> 3% of each run, Pallas kernels for 0% -> 0%
where the time goes in v1:
time: 169 us; the launch traced here: 167 us
  blocking collectives  92.6 us (55%)
  waiting for transfers between devices  27.2 us (16%)
  between operations  17.4 us (10%)
  Pallas kernels  11.5 us (7%)
  other arithmetic  7.47 us (4%)
  starting transfers between devices  6.57 us (4%)
  local copies, waits for them, and re-layouts  4.08 us (2%)
    all_gather x4, blocking collectives, local(): lax.all_gather(wide[:, q * chunk:(q + 1) * chunk], 'tensor', axis=0, tile...  53.9 us
    all_to_all x1, blocking collectives, local(): data = jnp.sum(lax.all_to_all(sums, 'dp', 0, 0, tiled=True), axis=0)  26 us
    all_gather x1, waiting for transfers between devices, local(): weight = lax.all_gather(packed, 'dp', axis=0, tiled=True)  23.4 us
    all_gather x1, blocking collectives, local(): lax.all_gather(dout, 'tensor', axis=0, tiled=True, axis_index_groups=alon...  12.7 us
    pallas_call x1, Pallas kernels, pre_grads(): pl.pallas_call(kernel, grid=(steps,), in_specs=[whole(r.shape) for r in r...  11.5 us
    all_to_all x1, starting transfers between devices, local(): lax.all_to_all(jnp.broadcast_to(mine, (tensor, LANE)), 'tensor', 0, 0, ti...  6.53 us
    all_to_all x1, waiting for transfers between devices, local(): lax.all_to_all(jnp.broadcast_to(mine, (tensor, LANE)), 'tensor', 0, 0, ti...  3.85 us
  transfers between devices with their start and end apart: 2, of which 2 were waited for; matrix products, arithmetic and copies ran while one was open for 3% of the time, Pallas kernels for 0%

profile of v1, /device:TPU:1, one launch (start us, length us, event | category | flops | bytes accessed | tf_op | source)
XLA Modules:
  0.0 167.4 jit_solution(8441786418478480754)
XLA Ops:
  7.2 0.0 copy-start.1
  7.2 0.0 copy-start.4
  7.2 0.0 copy-start.5
  7.2 0.0 all-gather.2.cloned.1.call-start
  7.2 1.8 %fusion.5 = bf16[160,1280]{1,0:T(8,128)(2,1)} fusion(bf16[160,864]{1,0:T(8,128)(2,1)} %bitcast.19, bf16[160,320]{1,0:T(8,128)(2,1)} %bitcast.21), kind=kLoop, calls=%fused_computation.10 | loop fusion | flops 1638400 | bytes 788480 | tf_op jit(solution)/shard_map/concatenate | solution.py:125
  9.1 0.0 all-gather.2.cloned.1.call-update
  9.1 1.3 fusion.15
  10.5 1.5 copy.25
  11.9 0.2 copy.24
  12.2 0.6 fusion.26
  12.8 0.3 fusion.6
  13.1 0.6 fusion.9.refs_6_
  13.7 1.0 fusion.2.refs_5_
  14.7 12.7 %all_gather.18 = bf16[96,5120]{1,0:T(8,128)(2,1)S(1)} all-gather(bf16[24,5120]{1,0:T(8,128)(2,1)S(1)} %copy-done), channel_id=1, replica_groups={{0,1,2,3},{4,5,6,7},{8,9,10,11},{12,13,14,15},{16,17,18,19},{20,21,22,2..., dimensions={0}, use_global_device_ids=true | all-gather | bytes 1228800 | tf_op jit(solution)/shard_map/all_gather | solution.py:128
  27.4 0.1 fusion.27
  27.5 13.9 %all_gather.19.refs_0_ = bf16[384,1280]{1,0:T(8,128)(2,1)} all-gather(bf16[96,1280]{1,0:T(8,128)(2,1)S(1)} %get-tuple-element.15), channel_id=1, replica_groups={{0,4,8,12},{1,5,9,13},{2,6,10,14},{3,7,11,15},{16,20,24,28},{17,21,25,2..., dimensions={0}, use_global_device_ids=true | all-gather | bytes 1228800 | tf_op jit(solution)/shard_map/all_gather | solution.py:131
  41.4 12.6 %all_gather.20.refs_1_ = bf16[384,1280]{1,0:T(8,128)(2,1)} all-gather(bf16[96,1280]{1,0:T(8,128)(2,1)S(1)} %get-tuple-element.14), channel_id=1, replica_groups={{0,4,8,12},{1,5,9,13},{2,6,10,14},{3,7,11,15},{16,20,24,28},{17,21,25,2..., dimensions={0}, use_global_device_ids=true | all-gather | bytes 1228800 | tf_op jit(solution)/shard_map/all_gather | solution.py:131
  53.9 14.5 %all_gather.21.refs_2_ = bf16[384,1280]{1,0:T(8,128)(2,1)} all-gather(bf16[96,1280]{1,0:T(8,128)(2,1)S(1)} %get-tuple-element.13), channel_id=1, replica_groups={{0,4,8,12},{1,5,9,13},{2,6,10,14},{3,7,11,15},{16,20,24,28},{17,21,25,2..., dimensions={0}, use_global_device_ids=true | all-gather | bytes 1228800 | tf_op jit(solution)/shard_map/all_gather | solution.py:131
  68.5 13.0 %all_gather.22.refs_3_ = bf16[384,1280]{1,0:T(8,128)(2,1)} all-gather(bf16[96,1280]{1,0:T(8,128)(2,1)S(1)} %get-tuple-element.12), channel_id=1, replica_groups={{0,4,8,12},{1,5,9,13},{2,6,10,14},{3,7,11,15},{16,20,24,28},{17,21,25,2..., dimensions={0}, use_global_device_ids=true | all-gather | bytes 1228800 | tf_op jit(solution)/shard_map/all_gather | solution.py:131
  81.4 23.4 %all-gather.2.cloned.1.call-done.refs_4_ = bf16[5120,1280]{1,0:T(8,128)(2,1)} async-done(((bf16[160,1280]{1,0:T(8,128)(2,1)}), bf16[5120,1280]{1,0:T(8,128)(2,1)}) %all-gather.2.cloned.1.call-update) | async-done | bytes 13107216 | tf_op jit(solution)/shard_map/all_gather | solution.py:126
  104.8 11.5 %pre_grads.1 = (bf16[320,384]{1,0:T(8,128)(2,1)}, bf16[864,384]{1,0:T(8,128)(2,1)}, f32[32,1280]{1,0:T(8,128)}) custom-call(bf16[384,1280]{1,0:T(8,128)(2,1)} %all_gather.19.refs_0_, bf16[384,1280]{1,0:T(8,128)(2,1)} %all_gather.20.refs_1_, bf16[384,1280]{1,0:T(8,128)(2,1)} %all_gather.21.refs_2_, bf16[384,1280]{1,0:T(8,128)(2,1)} %all_gather.22.refs_3_, ...), custom_call_target="tpu_custom_call" | custom-call | tf_op jit(solution)/shard_map/pre_grads/pallas_call | solution.py:75
  116.4 1.1 copy.26
  117.5 26.0 %all_to_all.15 = f32[32,1,1280]{2,1,0:T(1,128)S(1)} all-to-all(f32[32,1,1280]{2,1,0:T(1,128)S(1)} %copy.26), channel_id=1, replica_groups=mesh['dp'=32,'tensor'=16] {'dp'}, dimensions={0} | all-to-all | bytes 327680 | tf_op jit(solution)/shard_map/all_to_all | solution.py:155
  143.4 0.1 reduce_sum.36
  143.5 0.2 convolution_bitcast_fusion
  143.8 0.7 pad_maximum_fusion
  144.5 0.6 broadcast_in_dim.21
  145.1 6.5 %all-to-all-start.1 = ((f32[16,1,128]{2,1,0:T(1,128)}), f32[16,1,128]{2,1,0:T(1,128)S(1)}, u32[]{:S(2)}, u32[]{:S(2)}) async-start(f32[16,1,128]{2,1,0:T(1,128)} %broadcast_in_dim.21), calls=%async_computation.1 | async-start | bytes 16384 | tf_op jit(solution)/shard_map/all_to_all | solution.py:165
  154.2 3.8 %all-to-all-done.1 = f32[16,1,128]{2,1,0:T(1,128)S(1)} async-done(((f32[16,1,128]{2,1,0:T(1,128)}), f32[16,1,128]{2,1,0:T(1,128)S(1)}, u32[]{:S(2)}, u32[]{:S(2)}) %all-to-all-start.1) | async-done | bytes 8224 | tf_op jit(solution)/shard_map/all_to_all | solution.py:165
  158.1 0.6 slice.30
  159.4 0.6 fusion.10
  160.0 0.5 multiply_add_fusion.1
  (15 shorter events, 0.1 us)
Async XLA Ops:
  7.2 4.8 %copy-start.1 = (bf16[384,320]{0,1:T(8,128)(2,1)S(1)}, bf16[384,320]{0,1:T(8,128)(2,1)}, u32[]{:S(2)}) copy-start(bf16[384,320]{0,1:T(8,128)(2,1)} %param.13) | copy-start | bytes 737284
  7.2 5.0 %copy-start.4 = (f32[40]{0:T(128)S(1)}, f32[40]{0:T(128)}, u32[]{:S(2)}) copy-start(f32[40]{0:T(128)} %param.17) | copy-start | bytes 484
  7.2 5.0 %copy-start.5 = (f32[40]{0:T(128)S(1)}, f32[40]{0:T(128)}, u32[]{:S(2)}) copy-start(f32[40]{0:T(128)} %param.19) | copy-start | bytes 484
  7.2 97.6 %all-gather.2.cloned.1.call-start = ((), (), s32[]{:S(2)}) async-start(), calls=%async_computation.2 | async-start | bytes 13516800 | tf_op jit(solution)/shard_map/all_gather | solution.py:126
  10.5 4.3 %copy-start = (bf16[24,5120]{1,0:T(8,128)(2,1)S(1)}, bf16[24,5120]{1,0:T(8,128)(2,1)}, u32[]{:S(2)}) copy-start(bf16[24,5120]{1,0:T(8,128)(2,1)} %param.12) | copy-start | bytes 737284
  81.4 77.9 %copy-start.2 = (f32[864]{0:T(1024)S(1)}, f32[864]{0:T(1024)}, u32[]{:S(2)}) copy-start(f32[864]{0:T(1024)} %param.18) | copy-start | bytes 10372
  81.4 77.9 %copy-start.3 = (f32[864]{0:T(1024)S(1)}, f32[864]{0:T(1024)}, u32[]{:S(2)}) copy-start(f32[864]{0:T(1024)} %param.20) | copy-start | bytes 10372
  145.1 13.0 %all-to-all-start.1 = ((f32[16,1,128]{2,1,0:T(1,128)}), f32[16,1,128]{2,1,0:T(1,128)S(1)}, u32[]{:S(2)}, u32[]{:S(2)}) async-start(f32[16,1,128]{2,1,0:T(1,128)} %broadcast_in_dim.21), calls=%async_computation.1 | async-start | bytes 16384 | tf_op jit(solution)/shard_map/all_to_all | solution.py:165
Sparse Core Ops, SparseCore 0:
  10.7 94.0 all-gather.1

commit v2 on v1

v2 whole, which is shorter than its diff:
```python
import jax
import jax.numpy as jnp
from jax import lax
from jax.experimental import pallas as pl
from jax.experimental.pallas import tpu as pltpu
from jax.sharding import PartitionSpec as P

HEAD = 128
LANE = 128
TILE = 256

low_end = -0.1
high_end = 1.1
temper = 2.0 / 3.0


def concrete(logits, noise):
    shape_s = jax.nn.sigmoid((jnp.log(noise) - jnp.log(1.0 - noise) + logits) / temper)
    stretched = shape_s * (high_end - low_end) + low_end
    gate = jnp.clip(stretched, 0.0, 1.0)
    inside = jnp.logical_and(stretched > 0.0, stretched < 1.0)
    slope = jnp.where(
        inside, (high_end - low_end) / temper * shape_s * (1.0 - shape_s), 0.0 * shape_s
    )
    return (gate, slope)


def open_prob(logits):
    return jax.nn.sigmoid(logits - temper * jnp.log(-low_end / high_end))


def up(n, m):
    return -(-n // m) * m


def pad_to(x, n):
    return jnp.pad(x, ((0, 0), (0, n - x.shape[1])))


def column_sums(act, pre):
    return jnp.sum(act.astype(jnp.float32) * pre, axis=0, keepdims=True)


def fetch(weight, held, sems, first, count, parts):
    per = weight.shape[0] // parts
    copies = [
        [
            pltpu.make_async_copy(
                weight.at[pl.ds(q * per, per), first + j],
                held.at[j, pl.ds(q * per, per)],
                sems.at[j, q],
            )
            for q in range(parts)
        ]
        for j in range(count)
    ]
    for tile in copies:
        for c in tile:
            c.start()
    return copies


def product(rows, held, copies, j):
    shards, depth = held.shape[1], held.shape[2]
    per = shards // len(rows)
    pre = None
    for q, r in enumerate(rows):
        copies[j][q].wait()
        block = held[j, pl.ds(q * per, per)].reshape(per * depth, TILE)
        term = jnp.dot(r[...], block, preferred_element_type=jnp.float32)
        pre = term if pre is None else pre + term
    return pre


def gated(pre, gate):
    return (pre * gate).astype(jnp.bfloat16).T


def specs(n):
    return [pl.BlockSpec(memory_space=pltpu.VMEM) for _ in range(n)]


def held_scratch(weight, count, parts):
    return [
        pltpu.VMEM((count, weight.shape[0], weight.shape[2], TILE), weight.dtype),
        pltpu.SemaphoreType.DMA((count, parts)),
    ]


def context_part(rows, weight, act, gate, member, extra, n_ctx, n_hid, peers):
    tokens, cols = act.shape
    parts, count = len(rows), cols // TILE
    edge = up(n_ctx, LANE)
    rest = cols - edge

    def kernel(*refs):
        row_refs = refs[:parts]
        w, act_ref, gate_ref, member_ref, extra_ref = refs[parts : parts + 5]
        ctx_ref, hid_ref, sum_ref, head_ref, held, sems, out_buf, out_sem = refs[parts + 5 :]
        sent = pltpu.make_async_copy(out_buf, hid_ref.at[pl.ds(0, rest)], out_sem)
        copies = fetch(w, held, sems, 0, count, parts)
        sums = []
        for j in range(count):
            at = j * TILE
            pre = product(row_refs, held, copies, j)
            sums.append(column_sums(act_ref[:, pl.ds(at, TILE)], pre))
            out = gated(pre, gate_ref[:, pl.ds(at, TILE)])
            stop = min(at + TILE, n_ctx)
            ctx_ref[pl.ds(at, stop - at), :] = out[: stop - at]
            if at + TILE > edge:
                out_buf[...] = out[edge - at :]
                sent.start()
        line = jnp.concatenate(sums, axis=1)
        sum_ref[...] = line[:, edge:]
        part = jnp.dot(
            jnp.broadcast_to(line[:, :edge], (8, edge)),
            member_ref[...],
            precision=lax.Precision.HIGHEST,
            preferred_element_type=jnp.float32,
        )
        head_ref[...] = jnp.broadcast_to((part[:1] + extra_ref[...])[None], (peers, 1, LANE))
        sent.wait()

    return pl.pallas_call(
        kernel,
        in_specs=specs(parts) + [pl.BlockSpec(memory_space=pltpu.HBM)] + specs(4),
        out_specs=[
            pl.BlockSpec(),
            pl.BlockSpec(memory_space=pltpu.HBM),
            pl.BlockSpec(),
            pl.BlockSpec(),
        ],
        out_shape=[
            jax.ShapeDtypeStruct((n_ctx, tokens), jnp.bfloat16),
            jax.ShapeDtypeStruct((n_hid, tokens), jnp.bfloat16),
            jax.ShapeDtypeStruct((1, rest), jnp.float32),
            jax.ShapeDtypeStruct((peers, 1, LANE), jnp.float32),
        ],
        scratch_shapes=held_scratch(weight, count, parts)
        + [pltpu.VMEM((rest, tokens), jnp.bfloat16), pltpu.SemaphoreType.DMA],
        compiler_params=pltpu.CompilerParams(vmem_limit_bytes=12 * 2**20),
        name="context_part",
    )(*rows, weight, act, gate, member, extra)


def hidden_part(rows, weight, first, act, gate, begun, done):
    tokens, cols = act.shape
    parts, count = len(rows), cols // TILE
    n_hid = begun.shape[0]

    def kernel(*refs):
        row_refs = refs[:parts]
        w, act_ref, gate_ref, _, hid_ref, sum_ref, held, sems, out_buf, out_sems = refs[parts:]
        copies = fetch(w, held, sems, first, count, parts)
        sent = []
        for j in range(count):
            at = j * TILE
            pre = product(row_refs, held, copies, j)
            out = gated(pre, gate_ref[:, pl.ds(at, TILE)])
            size = min(TILE, n_hid - done - at)
            out_buf[j] = out
            sent.append(
                pltpu.make_async_copy(
                    out_buf.at[j, pl.ds(0, size)],
                    hid_ref.at[pl.ds(done + at, size)],
                    out_sems.at[j],
                )
            )
            sent[j].start()
            sum_ref[:, pl.ds(at, TILE)] = column_sums(act_ref[:, pl.ds(at, TILE)], pre)
        for c in sent:
            c.wait()

    return pl.pallas_call(
        kernel,
        in_specs=specs(parts)
        + [pl.BlockSpec(memory_space=pltpu.HBM)]
        + specs(2)
        + [pl.BlockSpec(memory_space=pltpu.HBM)],
        out_specs=[pl.BlockSpec(memory_space=pltpu.HBM), pl.BlockSpec()],
        out_shape=[
            jax.ShapeDtypeStruct((n_hid, tokens), jnp.bfloat16),
            jax.ShapeDtypeStruct((1, cols), jnp.float32),
        ],
        scratch_shapes=held_scratch(weight, count, parts)
        + [pltpu.VMEM((count, TILE, tokens), jnp.bfloat16), pltpu.SemaphoreType.DMA((count,))],
        input_output_aliases={parts + 3: 0},
        compiler_params=pltpu.CompilerParams(vmem_limit_bytes=16 * 2**20),
        name="hidden_part",
    )(*rows, weight, act, gate, begun)


def pack(w_ctx, w_hid, p_ctx, p_hid):
    depth, n_ctx = w_ctx.shape
    n_hid = w_hid.shape[1]

    def kernel(ctx_ref, hid_ref, out_ref):
        for at in range(0, p_ctx + p_hid, LANE):
            rows = pl.ds(at // TILE * depth, depth)
            src, lo, n = (ctx_ref, at, n_ctx) if at < p_ctx else (hid_ref, at - p_ctx, n_hid)
            size = min(LANE, n - lo)
            out_ref[rows, pl.ds(at % TILE, size)] = src[:, pl.ds(lo, size)]
            if size < LANE:
                out_ref[rows, pl.ds(at % TILE + size, LANE - size)] = jnp.zeros(
                    (depth, LANE - size), out_ref.dtype
                )

    return pl.pallas_call(
        kernel,
        out_shape=jax.ShapeDtypeStruct(((p_ctx + p_hid) // TILE * depth, TILE), w_ctx.dtype),
        compiler_params=pltpu.CompilerParams(vmem_limit_bytes=4 * 2**20),
        name="pack",
    )(w_ctx, w_hid)


def line_up(heads, first, second, copies):
    a, b = first.shape[1], second.shape[1]

    def kernel(heads_ref, first_ref, second_ref, out_ref):
        total = jnp.sum(heads_ref[...], axis=0)
        line = jnp.concatenate([first_ref[...], second_ref[...], total], axis=1)
        out_ref[...] = jnp.broadcast_to(line[None], (copies, 1, a + b + LANE))

    return pl.pallas_call(
        kernel,
        out_shape=jax.ShapeDtypeStruct((copies, 1, a + b + LANE), jnp.float32),
        compiler_params=pltpu.CompilerParams(vmem_limit_bytes=4 * 2**20),
        name="line_up",
    )(heads, first, second)


def make_local(dp, tensor):
    side = 4
    along_x = [[b * side + i for i in range(side)] for b in range(tensor // side)]
    along_y = [[b + side * i for i in range(tensor // side)] for b in range(side)]

    def local(
        dout,
        attn_ctx,
        mlp_hidden,
        w_out,
        w_down,
        head_logits,
        unit_logits,
        head_noise,
        unit_noise,
        linear_mult,
        square_mult,
        target,
    ):
        n_ctx = attn_ctx.shape[1]
        n_hid = mlp_hidden.shape[1]
        p_ctx, p_hid = up(n_ctx, LANE), up(n_hid, LANE)
        heads = head_logits.shape[0]

        packed = pack(w_out.T, w_down.T, p_ctx, p_hid)
        tiles = (p_ctx + p_hid) // TILE
        weight = lax.all_gather(packed, "dp", axis=0, tiled=True)
        weight = weight.reshape(dp, tiles, w_out.shape[1], TILE)
        weight = pltpu.with_memory_space_constraint(weight, pltpu.HBM)

        wide = lax.all_gather(dout, "tensor", axis=0, tiled=True, axis_index_groups=along_x)
        chunk = wide.shape[1] // 4
        rows = [
            lax.all_gather(
                wide[:, q * chunk : (q + 1) * chunk],
                "tensor",
                axis=0,
                tiled=True,
                axis_index_groups=along_y,
            )
            for q in range(4)
        ]

        head_gate, head_slope = concrete(head_logits, head_noise)
        unit_gate, unit_slope = concrete(unit_logits, unit_noise)
        tensor_index = lax.axis_index("tensor")
        columns = tensor_index * n_ctx + lax.iota(jnp.int32, n_ctx)
        owner = columns // HEAD
        member = (owner[:, None] == lax.iota(jnp.int32, heads)[None, :]).astype(jnp.float32)
        col_gate = jnp.dot(member, head_gate, precision=lax.Precision.HIGHEST)
        p_head = open_prob(head_logits)
        p_unit = open_prob(unit_logits)
        gate = jnp.concatenate(
            [pad_to(col_gate[None, :], p_ctx), pad_to(unit_gate[None, :], p_hid)], axis=1
        )
        act = jnp.concatenate([pad_to(attn_ctx, p_ctx), pad_to(mlp_hidden, p_hid)], axis=1)
        cut = up(p_ctx, TILE)
        member = jnp.pad(member, ((0, p_ctx - n_ctx), (0, LANE - heads)))
        extra = jnp.where(
            lax.broadcasted_iota(jnp.int32, (1, LANE), 1) == heads, jnp.sum(p_unit), 0.0
        )

        ctx_t, begun, first_sums, head_rows = context_part(
            rows, weight, act[:, :cut], gate[:, :cut], member, extra, n_ctx, n_hid, tensor
        )
        head_rows = lax.all_to_all(head_rows, "tensor", 0, 0, tiled=True)
        hid_t, second_sums = hidden_part(
            rows, weight, cut // TILE, act[:, cut:], gate[:, cut:], begun, cut - p_ctx
        )
        lines = line_up(head_rows, first_sums, second_sums, dp)
        data = jnp.sum(lax.all_to_all(lines, "dp", 0, 0, tiled=True), axis=(0, 1))
        unit_data = data[:n_hid]
        head_data = data[p_hid : p_hid + heads]
        unit_mass = data[p_hid + heads] / dp

        denom = 4.0 * HEAD * heads + 3.0 * n_hid * tensor
        size = 100.0 * (4.0 * HEAD * jnp.sum(p_head) + 3.0 * unit_mass) / denom
        factor = linear_mult[0] + 2.0 * square_mult[0] * (size - target[0])
        head_grad = head_data * head_slope + factor * (400.0 * HEAD / denom) * p_head * (
            1.0 - p_head
        )
        unit_grad = unit_data * unit_slope + factor * (300.0 / denom) * p_unit * (1.0 - p_unit)
        return (ctx_t.T, hid_t.T, head_grad, unit_grad)

    return local


def solution(mesh):
    placed = (
        P(("dp", "tensor"), None),
        P("dp", "tensor"),
        P("dp", "tensor"),
        P("tensor", "dp"),
        P("tensor", "dp"),
        P(),
        P("tensor"),
        P(),
        P("tensor"),
        P(),
        P(),
        P(),
    )
    return jax.shard_map(
        make_local(mesh.shape["dp"], mesh.shape["tensor"]),
        mesh=mesh,
        in_specs=placed,
        out_specs=(P("dp", "tensor"), P("dp", "tensor"), P(), P("tensor")),
        check_vma=False,
    )
```

time: 169 us -> 170 us (level)
  blocking collectives: 92.6 us -> 65.8 us
  starting transfers between devices: 6.57 us -> 15.9 us
  Pallas kernels: 11.5 us -> 18.2 us
  waiting for transfers between devices: 27.2 us -> 33.6 us
  local copies, waits for them, and re-layouts: 4.08 us -> 9.83 us
    all_to_all x1 -> x0, blocking collectives: 26 us -> none  [local(): data = jnp.sum(lax.all_to_all(sums, 'dp', 0, 0, tiled=True), axis=0)]
    all_to_all x1 -> x2, waiting for transfers between devices: 3.85 us -> 13.3 us  [the longest x1 13.3 us: local(): data = jnp.sum(lax.all_to_all(lines, 'dp', 0, 0, tiled=True), axis=(0, 1))]
    all_to_all x1 -> x2, starting transfers between devices: 6.53 us -> 15.8 us  [the longest x1 9.3 us: local(): data = jnp.sum(lax.all_to_all(lines, 'dp', 0, 0, tiled=True), axis=(0, 1))]
    unnamed x14 -> x16, local copies, waits for them, and re-layouts: 1.71 us -> 9.05 us
    pallas_call x1 -> x4, Pallas kernels: 11.5 us -> 18.2 us  [the longest x1 9.3 us: hidden_part(): pl.pallas_call(kernel, in_specs=specs(parts) + [pl.BlockSpec(memory_space...]
    all_gather x1, waiting for transfers between devices: 23.4 us -> 20.3 us  [local(): weight = lax.all_gather(packed, 'dp', axis=0, tiled=True)]
    concatenate x2 -> x0, other arithmetic: 2.58 us -> none  [the longest x1 1.85 us: local(): jnp.concatenate([pad_to(w_out.T, p_ctx), pad_to(w_down.T, p_hid)], axis=1)]
  transfers between devices with their start and end apart: 2 -> 3, of which waited for: 2 -> 2; matrix products, arithmetic and copies ran while one was open for 3% -> 5% of each run, Pallas kernels for 0% -> 6%
where the time goes in v2:
time: 170 us; the launch traced here: 169 us
  blocking collectives  65.8 us (39%)
  waiting for transfers between devices  33.6 us (20%)
  Pallas kernels  18.2 us (11%)
  between operations  17.4 us (10%)
  starting transfers between devices  15.9 us (9%)
  local copies, waits for them, and re-layouts  9.83 us (6%)
  other arithmetic  8.02 us (5%)
    all_gather x4, blocking collectives, local(): lax.all_gather(wide[:, q * chunk:(q + 1) * chunk], 'tensor', axis=0, tile...  52.9 us
    all_gather x1, waiting for transfers between devices, local(): weight = lax.all_gather(packed, 'dp', axis=0, tiled=True)  20.3 us
    all_to_all x1, waiting for transfers between devices, local(): data = jnp.sum(lax.all_to_all(lines, 'dp', 0, 0, tiled=True), axis=(0, 1))  13.3 us
    all_gather x1, blocking collectives, local(): lax.all_gather(dout, 'tensor', axis=0, tiled=True, axis_index_groups=alon...  12.9 us
    all_to_all x1, starting transfers between devices, local(): data = jnp.sum(lax.all_to_all(lines, 'dp', 0, 0, tiled=True), axis=(0, 1))  9.3 us
    pallas_call x1, Pallas kernels, hidden_part(): pl.pallas_call(kernel, in_specs=specs(parts) + [pl.BlockSpec(memory_space...  9.3 us
    unnamed x16, local copies, waits for them, and re-layouts  9.05 us
    pallas_call x1, Pallas kernels, context_part(): pl.pallas_call(kernel, in_specs=specs(parts) + [pl.BlockSpec(memory_space...  7.41 us
  transfers between devices with their start and end apart: 3, of which 2 were waited for; matrix products, arithmetic and copies ran while one was open for 5% of the time, Pallas kernels for 6%

profile of v2, /device:TPU:1, one launch (start us, length us, event | category | flops | bytes accessed | tf_op | source)
XLA Modules:
  0.0 169.0 jit_solution(14840983724950434001)
XLA Ops:
  7.2 0.9 copy-done.4
  8.2 0.9 copy-done.5
  9.1 0.8 pack.1
  9.9 1.3 fusion.7
  11.2 1.1 copy.17
  12.4 1.4 copy.18
  13.9 0.7 compare_select_fusion.1.refs_8_
  14.6 1.8 %fusion.19 = (f32[]{:T(128)}, f32[40]{0:T(128)}, f32[40]{0:T(128)S(1)}) fusion(f32[40]{0:T(128)} %param.17, f32[40]{0:T(128)} %param.19), kind=kLoop, calls=%fused_computation.41 | loop fusion | flops 479 | bytes 644 | tf_op jit(solution)/shard_map/reduce_sum | solution.py:308
  16.4 0.3 fusion.8
  16.7 0.3 copy-done.6
  17.0 0.1 iota_compare_fusion
  17.1 0.7 pad_convert_fusion.refs_7_
  17.8 0.8 fusion.1.refs_5_
  18.6 12.9 %all_gather.18 = bf16[96,5120]{1,0:T(8,128)(2,1)S(1)} all-gather(bf16[24,5120]{1,0:T(8,128)(2,1)} %param.12), channel_id=1, replica_groups={{0,1,2,3},{4,5,6,7},{8,9,10,11},{12,13,14,15},{16,17,18,19},{20,21,22,2..., dimensions={0}, use_global_device_ids=true | all-gather | bytes 1228800 | tf_op jit(solution)/shard_map/all_gather | solution.py:262
  31.6 13.8 %all_gather.22.refs_3_ = bf16[384,1280]{1,0:T(8,128)(2,1)S(1)} all-gather(bf16[96,1280]{1,0:T(8,128)(2,1)S(1)} %get-tuple-element.18), channel_id=1, replica_groups={{0,4,8,12},{1,5,9,13},{2,6,10,14},{3,7,11,15},{16,20,24,28},{17,21,25,2..., dimensions={0}, use_global_device_ids=true | all-gather | bytes 1228800 | tf_op jit(solution)/shard_map/all_gather | solution.py:265
  45.4 12.1 %all_gather.21.refs_2_ = bf16[384,1280]{1,0:T(8,128)(2,1)S(1)} all-gather(bf16[96,1280]{1,0:T(8,128)(2,1)S(1)} %get-tuple-element.19), channel_id=1, replica_groups={{0,4,8,12},{1,5,9,13},{2,6,10,14},{3,7,11,15},{16,20,24,28},{17,21,25,2..., dimensions={0}, use_global_device_ids=true | all-gather | bytes 1228800 | tf_op jit(solution)/shard_map/all_gather | solution.py:265
  57.5 13.9 %all_gather.20.refs_1_ = bf16[384,1280]{1,0:T(8,128)(2,1)S(1)} all-gather(bf16[96,1280]{1,0:T(8,128)(2,1)S(1)} %get-tuple-element.20), channel_id=1, replica_groups={{0,4,8,12},{1,5,9,13},{2,6,10,14},{3,7,11,15},{16,20,24,28},{17,21,25,2..., dimensions={0}, use_global_device_ids=true | all-gather | bytes 1228800 | tf_op jit(solution)/shard_map/all_gather | solution.py:265
  71.4 13.1 %all_gather.19.refs_0_ = bf16[384,1280]{1,0:T(8,128)(2,1)} all-gather(bf16[96,1280]{1,0:T(8,128)(2,1)S(1)} %get-tuple-element.21), channel_id=1, replica_groups={{0,4,8,12},{1,5,9,13},{2,6,10,14},{3,7,11,15},{16,20,24,28},{17,21,25,2..., dimensions={0}, use_global_device_ids=true | all-gather | bytes 1228800 | tf_op jit(solution)/shard_map/all_gather | solution.py:265
  84.5 20.3 %all-gather.2.cloned.1.call-done = bf16[25600,256]{1,0:T(8,128)(2,1)} async-done(((bf16[800,256]{1,0:T(8,128)(2,1)}), bf16[25600,256]{1,0:T(8,128)(2,1)}) %all-gather.2.cloned.1.call-update) | async-done | bytes 13107216 | tf_op jit(solution)/shard_map/all_gather | solution.py:258
  104.8 1.2 copy-done
  106.0 1.0 copy-done.2
  107.0 0.9 copy-done.3
  107.9 7.4 %context_part.1 = (bf16[320,384]{1,0:T(8,128)(2,1)}, bf16[864,384]{1,0:T(8,128)(2,1)}, f32[1,128]{1,0:T(1,128)S(1)}, f32[16,1,128]{2,1,0:T(1,128)}) custom-call(bf16[384,1280]{1,0:T(8,128)(2,1)S(1)} %copy-done, bf16[384,1280]{1,0:T(8,128)(2,1)S(1)} %all_gather.20.refs_1_, bf16[384,1280]{1,0:T(8,128)(2,1)S(1)} %all_gather.21.refs_2_, ...), custom_call_target="tpu_custom_call" | custom-call | tf_op jit(solution)/shard_map/context_part/pallas_call | solution.py:124
  115.3 6.5 %all-to-all-start = ((f32[16,1,128]{2,1,0:T(1,128)}), f32[16,1,128]{2,1,0:T(1,128)S(1)}, u32[]{:S(2)}, u32[]{:S(2)}) async-start(f32[16,1,128]{2,1,0:T(1,128)} %get-tuple-element.13), calls=%async_computation | async-start | bytes 16384 | tf_op jit(solution)/shard_map/all_to_all | solution.py:297
  121.9 1.2 copy-done.1
  123.1 9.3 %hidden_part.1 = (bf16[864,384]{1,0:T(8,128)(2,1)}, f32[1,768]{1,0:T(1,128)S(1)}) custom-call(bf16[384,1280]{1,0:T(8,128)(2,1)S(1)} %copy-done.1, bf16[384,1280]{1,0:T(8,128)(2,1)S(1)} %all_gather.20.refs_1_, bf16[384,1280]{1,0:T(8,128)(2,1)S(1)} %all_gather.21.refs_2_, bf16[384,1280]{1,0:T(8,128)(2,1)S(1)} %all_gather.22.refs_3_, ...), custom_call_target="tpu_custom_call", output_to_operand_aliasing={{0}: (7, {})} | custom-call | tf_op jit(solution)/shard_map/hidden_part/pallas_call | solution.py:174
  132.4 0.7 line_up.1
  133.1 9.3 %all-to-all-start.1 = ((f32[32,1,1024]{2,1,0:T(1,128)}), f32[32,1,1024]{2,1,0:T(1,128)S(1)}, u32[]{:S(2)}, u32[]{:S(2)}) async-start(f32[32,1,1024]{2,1,0:T(1,128)} %line_up.1), calls=%async_computation.1 | async-start | bytes 262144 | tf_op jit(solution)/shard_map/all_to_all | solution.py:302
  145.0 13.3 %all-to-all-done.1 = f32[32,1,1024]{2,1,0:T(1,128)S(1)} async-done(((f32[32,1,1024]{2,1,0:T(1,128)}), f32[32,1,1024]{2,1,0:T(1,128)S(1)}, u32[]{:S(2)}, u32[]{:S(2)}) %all-to-all-start.1) | async-done | bytes 131104 | tf_op jit(solution)/shard_map/all_to_all | solution.py:302
  158.3 0.6 slice.42
  159.6 1.3 multiply_add_fusion
  160.9 1.2 multiply_add_fusion.2
  (19 shorter events, 0.4 us)
Async XLA Ops:
  7.2 97.6 %all-gather.2.cloned.1.call-start = ((), (), s32[]{:S(2)}) async-start(), calls=%async_computation.2 | async-start | bytes 13516800 | tf_op jit(solution)/shard_map/all_gather | solution.py:258
  7.2 1.0 copy-start.4
  8.2 0.9 copy-start.5
  16.4 0.6 copy-start.6
  104.8 1.2 copy-start
  106.0 1.0 copy-start.2
  107.0 0.9 copy-start.3
  115.3 17.1 %all-to-all-start = ((f32[16,1,128]{2,1,0:T(1,128)}), f32[16,1,128]{2,1,0:T(1,128)S(1)}, u32[]{:S(2)}, u32[]{:S(2)}) async-start(f32[16,1,128]{2,1,0:T(1,128)} %get-tuple-element.13), calls=%async_computation | async-start | bytes 16384 | tf_op jit(solution)/shard_map/all_to_all | solution.py:297
  121.9 1.2 copy-start.1
  133.1 25.2 %all-to-all-start.1 = ((f32[32,1,1024]{2,1,0:T(1,128)}), f32[32,1,1024]{2,1,0:T(1,128)S(1)}, u32[]{:S(2)}, u32[]{:S(2)}) async-start(f32[32,1,1024]{2,1,0:T(1,128)} %line_up.1), calls=%async_computation.1 | async-start | bytes 262144 | tf_op jit(solution)/shard_map/all_to_all | solution.py:302
Sparse Core Ops, SparseCore 0:
  10.7 94.0 all-gather.1
